TPU v7x, 32 devices: a whole 2x2x4 slice. The times are simulated.
32 devices in a mesh: role: 2 (over core), seq: 4 (over z), tp: 4 (over y, x).
Axes of the slice: x: 2, y: 2, z: 4, core: 2. Of those that a mesh axis runs over, the one named last changes fastest.
Arguments:
- merger_hidden: bfloat16 [512, 5120], P(('role', 'seq'), 'tp'), may hold values from -6 to 6
- merger_out: bfloat16 [5120, 8192], P('tp', ('role', 'seq')), may hold values from -0.078125 to 0.078125
- row_position: int32 [512], P(('role', 'seq')), may hold values from -1 to 2047, as said below
- prompt_embeds: bfloat16 [2048, 8192], P(('role', 'seq'), 'tp'), may hold values from -300 to 300
- norm_gain: bfloat16 [8192], P('tp'), may hold values from 0.099609375 to 1.8984375
- query_weight: bfloat16 [8192, 4096], P(None, 'tp'), may hold values from -2.762136 to 2.762136
- key_weight: bfloat16 [8192, 512], P(None, 'tp'), may hold values from -0.06629126 to 0.06629126
- value_weight: bfloat16 [8192, 512], P(None, 'tp'), may hold values from -0.0625 to 0.0625
Outputs:
- stream: bfloat16 [2048, 8192], P(('role', 'seq'), 'tp')
- context: bfloat16 [2048, 4096], P(('role', 'seq'), 'tp')
Inputs may be any that keep to these rules, and one draw needn't show every extreme that they name: `row_position`: the live slots of each device's 64 come first and hold distinct prompt positions, distinct over all devices; the other slots hold -1. Of one device's slots at most 16 hold positions of one owner's block (positions j * 256 to (j + 1) * 256 - 1); every device has 16 or more live slots.
All inputs are finite; a program needn't handle non-finite values.
Results may differ from a plain program's by a relative error of at most 0.012.
The roundings to bfloat16 on the way count: a program that leaves them out, or rounds other values in their place, can miss the bound.
Values may be sent and summed in bfloat16 or wider, within the bound.
No kernel may reach another device: no remote copies, remote signals or barrier semaphores. Data moves between devices by JAX's collectives and lax.ppermute only.
A program may use at most 192 MiB of HBM per device.

v0:
```python
import math

import jax
import jax.numpy as jnp
from jax import lax
from jax.sharding import PartitionSpec as P

HEAD_DIM = 128


def rotate(vectors, positions):
    half_dim = vectors.shape[-1] // 2
    frequency = 1000000.0 ** (-jnp.arange(half_dim, dtype=jnp.float32) / half_dim)
    angles = positions.astype(jnp.float32)[:, None, None] * frequency[None, None, :]
    cosine = jnp.cos(angles)
    sine_part = jnp.sin(angles)
    lower_half = vectors[..., :half_dim]
    upper_half = vectors[..., half_dim:]
    return jnp.concatenate(
        [
            lower_half * cosine - upper_half * sine_part,
            upper_half * cosine + lower_half * sine_part,
        ],
        axis=-1,
    )


def sum_hidden(partial_value):
    return lax.psum_scatter(partial_value, "tp", scatter_dimension=1, tiled=True).astype(
        jnp.bfloat16
    )


def project_strips(merger_hidden, merger_out):
    return jnp.dot(
        lax.all_gather(merger_hidden, ("role", "seq"), axis=0, tiled=True),
        merger_out,
        preferred_element_type=jnp.float32,
    )


def body(
    merger_hidden,
    merger_out,
    row_position,
    prompt_embeds,
    norm_gain,
    query_weight,
    key_weight,
    value_weight,
):
    groups = lax.axis_size("role") * lax.axis_size("seq")
    device_rank = lax.axis_index(("role", "seq"))
    row_count = merger_hidden.shape[0]
    tok_count = prompt_embeds.shape[0]
    columns = prompt_embeds.shape[1]
    model_width = columns * lax.axis_size("tp")
    capacity = 2 * row_count // groups
    strips = project_strips(merger_hidden, merger_out)
    partial_value = lax.all_to_all(strips, ("role", "seq"), split_axis=0, concat_axis=1, tiled=True)
    embeds = sum_hidden(partial_value)
    owners = jnp.where(row_position >= 0, row_position // tok_count, groups)
    onehot = (owners[:, None] == jnp.arange(groups, dtype=jnp.int32)[None, :]).astype(jnp.int32)
    earlier = jnp.sum((jnp.cumsum(onehot, axis=0) - onehot) * onehot, axis=1)
    buffer_slot = jnp.where(owners < groups, owners * capacity + earlier, groups * capacity)
    source = (
        jnp.full((groups * capacity,), row_count, jnp.int32)
        .at[buffer_slot]
        .set(jnp.arange(row_count, dtype=jnp.int32), mode="drop")
    )
    padded = jnp.concatenate([embeds, jnp.zeros((1, columns), jnp.bfloat16)], axis=0)
    outgoing = padded[source].reshape(groups, capacity, columns)
    outgoing_pos = jnp.concatenate([row_position, jnp.full((1,), -1, jnp.int32)])[source].reshape(
        groups, capacity
    )
    arrived, arrived_pos = (
        lax.all_to_all(outgoing, ("role", "seq"), split_axis=0, concat_axis=0, tiled=True),
        lax.all_to_all(outgoing_pos, ("role", "seq"), split_axis=0, concat_axis=0, tiled=True),
    )
    arrived_pos = arrived_pos.reshape(-1)
    local_row = jnp.where(arrived_pos >= 0, arrived_pos - device_rank * tok_count, tok_count)
    stream = prompt_embeds.at[local_row].set(arrived.reshape(-1, columns), mode="drop")
    widened = stream.astype(jnp.float32)
    squares = lax.psum(jnp.sum(widened * widened, axis=1), "tp")
    inverse = lax.rsqrt(squares / model_width + 1e-06)[:, None]
    normed = (widened * inverse * norm_gain.astype(jnp.float32)[None, :]).astype(jnp.bfloat16)
    tables = (query_weight, key_weight, value_weight)
    shard_piece = lax.all_gather(normed, "tp", axis=1, tiled=True)
    query_sum, key_sum, value_sum = tuple(
        (jnp.dot(shard_piece, table, preferred_element_type=jnp.float32) for table in tables)
    )
    local_heads = query_weight.shape[1] // HEAD_DIM
    local_kv = key_weight.shape[1] // HEAD_DIM
    group_size = local_heads // local_kv
    positions = device_rank * tok_count + jnp.arange(tok_count, dtype=jnp.int32)
    queries = rotate(query_sum.reshape(tok_count, local_heads, HEAD_DIM), positions).astype(
        jnp.bfloat16
    )
    queries = queries.reshape(tok_count, local_kv, group_size, HEAD_DIM)
    key_rows = rotate(key_sum.reshape(tok_count, local_kv, HEAD_DIM), positions).astype(
        jnp.bfloat16
    )
    value_rows = value_sum.astype(jnp.bfloat16).reshape(tok_count, local_kv, HEAD_DIM)
    score_scale = 1.0 / math.sqrt(HEAD_DIM)
    running_max = jnp.full((local_kv, group_size, tok_count), -1e30, jnp.float32)
    key_piece = lax.all_gather(key_rows, ("role", "seq"), axis=0, tiled=True)
    value_piece = lax.all_gather(value_rows, ("role", "seq"), axis=0, tiled=True)
    scores = (
        jnp.einsum("qhgd,khd->hgqk", queries, key_piece, preferred_element_type=jnp.float32)
        * score_scale
    )
    key_pos = jnp.arange(key_piece.shape[0], dtype=jnp.int32)
    visible = key_pos[None, :] <= positions[:, None]
    scores = jnp.where(visible, scores, -jnp.inf)
    next_max = jnp.maximum(running_max, jnp.max(scores, axis=3))
    probability = jnp.where(visible, jnp.exp(scores - next_max[..., None]), 0.0)
    running_sum = jnp.sum(probability, axis=3)
    running_out = jnp.einsum(
        "hgqk,khd->hgqd",
        probability.astype(jnp.bfloat16),
        value_piece,
        preferred_element_type=jnp.float32,
    )
    running_max, running_sum, running_out = (next_max, running_sum, running_out)
    context = running_out / running_sum[..., None]
    context = (
        jnp.transpose(context, (2, 0, 1, 3))
        .reshape(tok_count, local_heads * HEAD_DIM)
        .astype(jnp.bfloat16)
    )
    return (stream, context)


def solution(mesh):
    in_specs = (
        P(("role", "seq"), "tp"),
        P("tp", ("role", "seq")),
        P(("role", "seq")),
        P(("role", "seq"), "tp"),
        P("tp"),
        P(None, "tp"),
        P(None, "tp"),
        P(None, "tp"),
    )
    out_specs = (P(("role", "seq"), "tp"), P(("role", "seq"), "tp"))
    return jax.shard_map(body, mesh=mesh, in_specs=in_specs, out_specs=out_specs, check_vma=False)
```

profile of v0, /device:TPU:0, one launch (start us, length us, event | category | flops | bytes accessed | tf_op | source)
XLA Modules:
  0.0 304.1 jit_solution(15773914192989135023)
XLA Ops:
  7.2 0.0 copy-start
  7.2 0.0 all-gather.4.cloned.1.call-start
  7.2 2.5 copy.45
  9.7 0.0 all-gather.4.cloned.1.call-update
  9.7 0.0 reduce-scatter.2.cloned.1.call-start
  9.8 26.2 %all-gather.4.cloned.1.call-done = bf16[512,1280]{1,0:T(8,128)(2,1)} async-done(((bf16[64,1280]{1,0:T(8,128)(2,1)}), bf16[512,1280]{1,0:T(8,128)(2,1)}) %all-gather.4.cloned.1.call-update) | async-done | bytes 1310736 | tf_op jit(solution)/shard_map/all_gather | solution.py:36
  36.0 0.0 copy-done
  36.0 2.8 fusion.37
  38.8 51.7 %all_to_all.33 = f32[8,64,1024]{2,1,0:T(8,128)S(1)} all-to-all(f32[8,64,1024]{2,1,0:T(8,128)S(1)} %bitcast.65), channel_id=1, replica_groups=mesh['role'=2,'seq'=4,'tp'=4] {'role','seq'}, dimensions={0} | all-to-all | bytes 4194304 | tf_op jit(solution)/shard_map/all_to_all | solution.py:60
  90.5 0.0 copy-start.4
  90.5 1.5 copy.37
  92.0 0.0 reduce-scatter.2.cloned.1.call-update
  92.1 0.0 copy-done.4
  92.1 0.0 copy-start.3
  92.1 0.1 fusion.26
  92.2 0.1 reduce_window_sum.11
  92.3 0.2 select_reduce_fusion
  92.5 0.8 scatter_custom_fusion
  93.3 0.1 pad_add_fusion
  93.3 1.2 gather_fusion
  94.6 0.7 all_to_all.23
  95.2 3.3 %all-to-all-start = ((s32[8,1,16]{2,1,0:T(1,128)}), s32[8,1,16]{2,1,0:T(1,128)S(1)}, u32[]{:S(2)}, u32[]{:S(2)}) async-start(s32[8,1,16]{2,1,0:T(1,128)} %bitcast), calls=%async_computation | async-start | bytes 8192 | tf_op jit(solution)/shard_map/all_to_all | solution.py:78
  98.5 27.3 %reduce-scatter.2.cloned.1.call-done = f32[64,2048]{1,0:T(8,128)} async-done(((f32[64,8192]{1,0:T(8,128)}), f32[64,2048]{1,0:T(8,128)}) %reduce-scatter.2.cloned.1.call-update) | async-done | bytes 524304 | tf_op jit(solution)/shard_map/reduce_scatter | solution.py:29
  125.9 1.1 convert_element_type.54
  127.0 1.7 gather_fusion.1
  128.7 0.0 all-to-all-done
  128.7 4.6 %all-to-all-start.2 = ((bf16[8,16,2048]{2,1,0:T(8,128)(2,1)}), bf16[8,16,2048]{2,1,0:T(8,128)(2,1)S(1)}, u32[]{:S(2)}, u32[]{:S(2)}) async-start(bf16[8,16,2048]{2,1,0:T(8,128)(2,1)} %bitcast.4), calls=%async_computation.3 | async-start | bytes 1048576 | tf_op jit(solution)/shard_map/all_to_all | solution.py:77
  133.3 0.0 all-gather.6.cloned.1.call-start
  133.3 0.0 copy-done.3
  133.4 0.1 select_n.56
  133.5 14.6 %all-to-all-done.2 = bf16[8,16,2048]{2,1,0:T(8,128)(2,1)S(1)} async-done(((bf16[8,16,2048]{2,1,0:T(8,128)(2,1)}), bf16[8,16,2048]{2,1,0:T(8,128)(2,1)S(1)}, u32[]{:S(2)}, u32[]{:S(2)}) %all-to-all-start.2) | async-done | bytes 524320 | tf_op jit(solution)/shard_map/all_to_all | solution.py:77
  148.0 3.7 %scatter_fusion = bf16[256,2048]{1,0:T(8,128)(2,1)} fusion(bf16[256,2048]{1,0:T(8,128)(2,1)} %copy.45, s32[128]{0:T(128)S(1)} %fusion.28, bf16[128,2048]{1,0:T(8,128)(2,1)S(1)} %bitcast.64), kind=kCustom, calls=%fused_computation.3 | custom fusion | bytes 1573376 | tf_op jit(solution)/shard_map/scatter | solution.py:82
  151.7 1.5 fusion.7
  153.2 8.9 %psum.7 = f32[256]{0:T(256)S(1)} all-reduce(f32[256]{0:T(256)S(1)} %fusion.7), channel_id=1, replica_groups=mesh['role'=2,'seq'=4,'tp'=4] {'tp'}, use_global_device_ids=true, to_apply=%region_6.7 | all-reduce | flops 256 | bytes 2048 | tf_op jit(solution)/shard_map/psum | solution.py:84
  162.2 2.5 fusion.9
  164.7 0.0 all-gather.6.cloned.1.call-update
  164.7 0.5 multiply_cosine_fusion
  165.3 0.3 iota_compare_fusion
  165.6 49.5 %all-gather.6.cloned.1.call-done = bf16[256,8192]{1,0:T(8,128)(2,1)} async-done(((bf16[256,2048]{1,0:T(8,128)(2,1)}), bf16[256,8192]{1,0:T(8,128)(2,1)}) %all-gather.6.cloned.1.call-update) | async-done | bytes 4194320 | tf_op jit(solution)/shard_map/all_gather | solution.py:88
  215.1 0.0 copy-start.1
  215.1 4.5 %convolution_bitcast_fusion.1 = f32[256,1,128]{0,2,1:T(8,128)S(1)} fusion(bf16[256,8192]{1,0:T(8,128)(2,1)} %all-gather.6.cloned.1.call-done, bf16[8192,128]{1,0:T(8,128)(2,1)} %param.14), kind=kOutput, calls=%fused_computation.19 | convolution fusion | flops 536870912 | bytes 6422528 | tf_op jit(solution)/shard_map/dot_general | solution.py:90
  219.6 0.3 fusion.23
  219.9 0.0 copy-done.1
  219.9 0.0 copy-start.2
  219.9 8.4 %convolution_bitcast_fusion = f32[32,8,8,128]{3,1,2,0:T(8,128)S(1)} fusion(bf16[256,8192]{1,0:T(8,128)(2,1)S(1)} %copy-done.1, bf16[8192,1024]{1,0:T(8,128)(2,1)} %param.13), kind=kOutput, calls=%fused_computation.18 | convolution fusion | flops 4294967296 | bytes 22020096 | tf_op jit(solution)/shard_map/dot_general | solution.py:90
  228.4 0.2 copy.38
  228.6 26.5 %all_gather.14 = bf16[2048,1,128]{0,2,1:T(8,128)(2,1)S(1)} all-gather(bf16[256,1,128]{0,2,1:T(8,128)(2,1)S(1)} %pad_maximum_fusion), channel_id=1, replica_groups=mesh['role'=2,'seq'=4,'tp'=4] {'role','seq'}, dimensions={0}, use_global_device_ids=true | all-gather | bytes 589824 | tf_op jit(solution)/shard_map/all_gather | solution.py:106
  255.1 0.0 copy-done.2
  255.1 1.2 convolution_convert_fusion
  256.3 26.6 %all-gather = bf16[2048,128]{1,0:T(8,128)(2,1)S(1)} all-gather(bf16[256,128]{1,0:T(8,128)(2,1)S(1)} %convolution_convert_fusion), channel_id=2, replica_groups=mesh['role'=2,'seq'=4,'tp'=4] {'role','seq'}, dimensions={0}, use_global_device_ids=true | all-gather | bytes 589824 | tf_op jit(solution)/shard_map/all_gather | solution.py:107
  283.0 0.3 fusion.36
  283.3 0.4 subtract_convert_fusion
  283.7 2.8 fusion
  286.6 4.0 %fusion.1 = f32[8,256]{1,0:T(8,128)S(1)} fusion(f32[2048,256,8]{1,0,2:T(8,128)S(1)} %get-tuple-element.17, f32[8,256]{1,0:T(8,128)S(1)} %broadcast_maximum_fusion, pred[256,2048]{0,1:T(8,128)(4,1)S(1)} %iota_compare_fusion), kind=kLoop, calls=%fused_computation.7 | loop fusion | flops 20969472 | bytes 17317888 | tf_op jit(solution)/shard_map/reduce_sum | solution.py:117
  290.6 4.9 %divide_convert_fusion = bf16[8,256,128]{1,2,0:T(8,128)(2,1)} fusion(f32[2048,256,8]{1,0,2:T(8,128)S(1)} %get-tuple-element.17, f32[8,256]{1,0:T(8,128)S(1)} %broadcast_maximum_fusion, pred[256,2048]{0,1:T(8,128)(4,1)S(1)} %iota_compare_fusion, bf16[2048,128]{1,0:T(8,128)(2,1)S(1)} %all-gather, f32[8,256]{1,0:T(8,128)S(1)} %fusion.1), kind=kOutput, calls=%fused_computation.21 | convolution fusion | flops 1095237632 | bytes 18366464 | tf_op jit(solution)/shard_map/hgqk,khd->hgqd/dot_general | solution.py:118
  295.5 2.0 copy.29
  (15 shorter events, 0.1 us)
Async XLA Ops:
  7.2 28.8 %copy-start = (bf16[1280,1024]{1,0:T(8,128)(2,1)S(1)}, bf16[1280,1024]{1,0:T(8,128)(2,1)}, u32[]{:S(2)}) copy-start(bf16[1280,1024]{1,0:T(8,128)(2,1)} %param.9) | copy-start | bytes 7864324
  7.2 28.8 %all-gather.4.cloned.1.call-start = ((), (), s32[]{:S(2)}) async-start(), calls=%async_computation.4 | async-start | bytes 1474560 | tf_op jit(solution)/shard_map/all_gather | solution.py:36
  9.7 116.1 %reduce-scatter.2.cloned.1.call-start = ((), (), s32[]{:S(2)}) async-start(), calls=%async_computation.5 | async-start | bytes 2621440 | tf_op jit(solution)/shard_map/reduce_scatter | solution.py:29
  90.5 1.5 copy-start.4
  92.1 41.3 %copy-start.3 = (bf16[2048]{0:T(1024)(128)(2,1)S(1)}, bf16[2048]{0:T(1024)(128)(2,1)}, u32[]{:S(2)}) copy-start(bf16[2048]{0:T(1024)(128)(2,1)} %param.12) | copy-start | bytes 12292
  95.2 33.4 %all-to-all-start = ((s32[8,1,16]{2,1,0:T(1,128)}), s32[8,1,16]{2,1,0:T(1,128)S(1)}, u32[]{:S(2)}, u32[]{:S(2)}) async-start(s32[8,1,16]{2,1,0:T(1,128)} %bitcast), calls=%async_computation | async-start | bytes 8192 | tf_op jit(solution)/shard_map/all_to_all | solution.py:78
  128.7 19.4 %all-to-all-start.2 = ((bf16[8,16,2048]{2,1,0:T(8,128)(2,1)}), bf16[8,16,2048]{2,1,0:T(8,128)(2,1)S(1)}, u32[]{:S(2)}, u32[]{:S(2)}) async-start(bf16[8,16,2048]{2,1,0:T(8,128)(2,1)} %bitcast.4), calls=%async_computation.3 | async-start | bytes 1048576 | tf_op jit(solution)/shard_map/all_to_all | solution.py:77
  133.3 81.8 %all-gather.6.cloned.1.call-start = ((), (), s32[]{:S(2)}) async-start(), calls=%async_computation.6 | async-start | bytes 5242880 | tf_op jit(solution)/shard_map/all_gather | solution.py:88
  215.1 4.8 %copy-start.1 = (bf16[256,8192]{1,0:T(8,128)(2,1)S(1)}, bf16[256,8192]{1,0:T(8,128)(2,1)}, u32[]{:S(2)}) copy-start(bf16[256,8192]{1,0:T(8,128)(2,1)} %all-gather.6.cloned.1.call-done) | copy-start | bytes 12582916
  219.9 35.2 %copy-start.2 = (bf16[8192,128]{1,0:T(8,128)(2,1)S(1)}, bf16[8192,128]{1,0:T(8,128)(2,1)}, u32[]{:S(2)}) copy-start(bf16[8192,128]{1,0:T(8,128)(2,1)} %param.15) | copy-start | bytes 6291460
Sparse Core Ops, SparseCore 0:
  9.8 26.1 all-gather.3
  92.2 33.6 reduce-scatter.1
  164.8 50.2 all-gather.5
where the time goes:
time: 305 us; the launch traced here: 304 us
  waiting for transfers between devices  118 us (39%)
  blocking collectives  114 us (37%)
  matrix products  24.7 us (8%)
  local copies, waits for them, and re-layouts  14.7 us (5%)
  between operations  14 us (5%)
  other arithmetic  11.2 us (4%)
  starting transfers between devices  7.98 us (3%)
    all_to_all x1, blocking collectives, body(): lax.all_to_all(strips, ('role', 'seq'), split_axis=0, concat_axis=1, tile...  51.7 us
    all_gather x1, waiting for transfers between devices, body(): shard_piece = lax.all_gather(normed, 'tp', axis=1, tiled=True)  49.5 us
    reduce_scatter x1, waiting for transfers between devices, sum_hidden(): lax.psum_scatter(partial_value, 'tp', scatter_dimension=1, tiled=True)  27.3 us
    all_gather x1, blocking collectives, body(): lax.all_gather(value_rows, ('role', 'seq'), axis=0, tiled=True)  26.6 us
    all_gather x1, blocking collectives, body(): key_piece = lax.all_gather(key_rows, ('role', 'seq'), axis=0, tiled=True)  26.5 us
    all_gather x1, waiting for transfers between devices, project_strips(): lax.all_gather(merger_hidden, ('role', 'seq'), axis=0, tiled=True)  26.2 us
    all_to_all x1, waiting for transfers between devices, body(): lax.all_to_all(outgoing, ('role', 'seq'), split_axis=0, concat_axis=0, ti...  14.6 us
    dot_general x3, matrix products, body(): jnp.dot(shard_piece, table, preferred_element_type=jnp.float32)  14.2 us
  transfers between devices with their start and end apart: 5, of which 4 were waited for; matrix products, arithmetic and copies ran while one was open for 2% of the time, Pallas kernels for 0%

commit v1 on v0

v1 whole, which is shorter than its diff:
```python
import functools
import math

import jax
import jax.numpy as jnp
from jax import lax
from jax.experimental import pallas as pl
from jax.experimental.pallas import tpu as pltpu
from jax.sharding import PartitionSpec as P

HEAD_DIM = 128
BF16 = jnp.bfloat16
F32 = jnp.float32


def swap(x, axis, k, keep=None):
    n = lax.axis_size(axis)
    pairs = [(i, i ^ k) for i in range(n) if keep is None or keep(i, i ^ k)]
    return lax.ppermute(x, axis, pairs)


def gather_xor(x, axis):
    return [x] + [swap(x, axis, k) for k in range(1, lax.axis_size(axis))]


def dot(a, b):
    return jnp.dot(a, b, preferred_element_type=F32)


def qkv_kernel(
    tp,
    groups,
    info,
    early_own,
    early_in,
    late_own,
    late_in,
    gain,
    cosine,
    sine,
    wq,
    wk,
    wv,
    q_out,
    kv_out,
    late_out,
    rows,
    inverse,
    acc,
):
    step = pl.program_id(0)
    me = info[0]
    early, columns = early_own.shape
    late = late_own.shape[0]
    width = rows.shape[1]
    strip = width // groups
    part = columns // groups
    q_cols, k_cols = wq.shape[1], wk.shape[1]
    v_cols = wv.shape[1]

    @pl.when(step == 0)
    def _():
        image_rows = lax.broadcasted_iota(jnp.int32, (late, 1), 0) < info[1]
        for k in range(tp):
            source = me ^ k
            base = pl.multiple_of(source * columns, columns)
            early_piece = early_own[...] if k == 0 else early_in[k - 1]
            rows[0:early, pl.ds(base, columns)] = early_piece
            late_piece = late_own[...] if k == 0 else late_in[k - 1]
            rows[early:, pl.ds(base, columns)] = late_piece
        for k in range(tp if part % 128 == 0 else 0):
            source = me ^ k
            for m in range(groups):
                at = pl.multiple_of(info[2 + m] * strip + source * part, part)
                if k == 0:
                    piece = late_own[:, m * part : (m + 1) * part]
                else:
                    piece = late_in[k - 1, :, m * part : (m + 1) * part]
                rows[early:, pl.ds(at, part)] = jnp.where(
                    image_rows, piece, rows[early:, pl.ds(at, part)]
                )
        late_out[...] = rows[early:, pl.ds(pl.multiple_of(me * columns, columns), columns)]
        total = jnp.zeros((early + late, 1), F32)
        for j in range(groups):
            piece = rows[:, j * strip : (j + 1) * strip].astype(F32)
            total = total + jnp.sum(piece * piece, axis=1, keepdims=True)
        inverse[...] = lax.rsqrt(total / width + 1e-06)
        acc[...] = jnp.zeros_like(acc)

    chunk = wq.shape[0]
    at = pl.multiple_of(step * chunk, chunk)
    scaled = rows[:, pl.ds(at, chunk)].astype(F32) * inverse[...]
    source = (step * chunk) // columns
    inner = pl.multiple_of(step * chunk - source * columns, chunk)
    weight = gain[me ^ source, :, pl.ds(inner, chunk)]
    normed = (scaled * weight).astype(BF16)
    acc[:, 0:q_cols] += dot(normed, wq[...])
    acc[:, q_cols : q_cols + k_cols] += dot(normed, wk[...])
    acc[:, q_cols + k_cols :] += dot(normed, wv[...])

    @pl.when(step == pl.num_programs(0) - 1)
    def _():
        half = HEAD_DIM // 2
        for head in range((q_cols + k_cols) // HEAD_DIM):
            first = head * HEAD_DIM
            vector = acc[:, first : first + HEAD_DIM]
            turned = jnp.concatenate([vector[:, half:], vector[:, :half]], axis=1)
            result = (vector * cosine[...] + turned * sine[...]).astype(BF16)
            if first < q_cols:
                q_out[:, first : first + HEAD_DIM] = result
            else:
                kv_out[:, first - q_cols : first - q_cols + HEAD_DIM] = result
        kv_out[:, k_cols : k_cols + v_cols] = acc[:, q_cols + k_cols :].astype(BF16)


def project(info, early_own, early_in, late_own, late_in, gain, cosine, sine, wq, wk, wv, groups):
    tp = early_in.shape[0] + 1
    early, columns = early_own.shape
    late = late_own.shape[0]
    tokens = early + late
    width = wq.shape[0]
    chunk = width // 8
    total = wq.shape[1] + wk.shape[1] + wv.shape[1]
    whole = lambda shape: pl.BlockSpec(shape, lambda j, info: (0,) * len(shape))
    return pl.pallas_call(
        functools.partial(qkv_kernel, tp, groups),
        grid_spec=pltpu.PrefetchScalarGridSpec(
            num_scalar_prefetch=1,
            grid=(width // chunk,),
            in_specs=[
                whole(early_own.shape),
                whole(early_in.shape),
                whole(late_own.shape),
                whole(late_in.shape),
                whole(gain.shape),
                whole(cosine.shape),
                whole(sine.shape),
                pl.BlockSpec((chunk, wq.shape[1]), lambda j, info: (j, 0)),
                pl.BlockSpec((chunk, wk.shape[1]), lambda j, info: (j, 0)),
                pl.BlockSpec((chunk, wv.shape[1]), lambda j, info: (j, 0)),
            ],
            out_specs=[
                whole((tokens, wq.shape[1])),
                whole((tokens, wk.shape[1] + wv.shape[1])),
                whole((late, columns)),
            ],
            scratch_shapes=[
                pltpu.VMEM((tokens, width), BF16),
                pltpu.VMEM((tokens, 1), F32),
                pltpu.VMEM((tokens, total), F32),
            ],
        ),
        out_shape=[
            jax.ShapeDtypeStruct((tokens, wq.shape[1]), BF16),
            jax.ShapeDtypeStruct((tokens, wk.shape[1] + wv.shape[1]), BF16),
            jax.ShapeDtypeStruct((late, columns), BF16),
        ],
        compiler_params=pltpu.CompilerParams(vmem_limit_bytes=48 << 20),
    )(info, early_own, early_in, late_own, late_in, gain, cosine, sine, wq, wk, wv)


def attention_kernel(pieces, group_size, blocks, q, *refs):
    kv_refs = refs[:pieces]
    q_pos, k_pos, place, out, scores = refs[pieces:]
    tokens = q.shape[0]
    scale = 1.0 / math.sqrt(HEAD_DIM)
    rank = blocks[0]
    top = None
    for j in range(pieces):
        keys = kv_refs[j][:, 0:HEAD_DIM]
        piece = lax.dot_general(
            q[...], keys, (((1,), (1,)), ((), ())), preferred_element_type=F32
        )
        piece = piece * scale
        if j == 0:
            piece = jnp.where(k_pos[...] <= q_pos[...], piece, -jnp.inf)
        else:
            piece = jnp.where(blocks[j] < rank, piece, -jnp.inf)
        scores[:, j * tokens : (j + 1) * tokens] = piece
        here = jnp.max(piece, axis=1, keepdims=True)
        top = here if top is None else jnp.maximum(top, here)
    total = None
    mixed = None
    for j in range(pieces):
        weight = jnp.exp(scores[:, j * tokens : (j + 1) * tokens] - top)
        here = jnp.sum(weight, axis=1, keepdims=True)
        total = here if total is None else total + here
        part = dot(weight.astype(BF16), kv_refs[j][:, HEAD_DIM:])
        mixed = part if mixed is None else mixed + part
    result = (mixed / total).astype(BF16)
    out[...] = dot(place[...], result).astype(BF16)


def attend(blocks, q, kvs, q_pos, k_pos, place, local_kv):
    tokens = q.shape[0]
    heads = q.shape[1] // HEAD_DIM
    group_size = heads // local_kv
    kv_spec = pl.BlockSpec((tokens, 2 * HEAD_DIM), lambda h, b: (0, h // group_size))
    whole = lambda shape: pl.BlockSpec(shape, lambda h, b: (0,) * len(shape))
    return pl.pallas_call(
        functools.partial(attention_kernel, len(kvs), group_size),
        grid_spec=pltpu.PrefetchScalarGridSpec(
            num_scalar_prefetch=1,
            grid=(heads,),
            in_specs=[pl.BlockSpec((tokens, HEAD_DIM), lambda h, b: (0, h))]
            + [kv_spec] * len(kvs)
            + [whole(q_pos.shape), whole(k_pos.shape), whole(place.shape)],
            out_specs=pl.BlockSpec((tokens, HEAD_DIM), lambda h, b: (0, h)),
            scratch_shapes=[pltpu.VMEM((tokens, tokens * len(kvs)), F32)],
        ),
        out_shape=jax.ShapeDtypeStruct(q.shape, BF16),
        compiler_params=pltpu.CompilerParams(vmem_limit_bytes=32 << 20),
    )(blocks, q, *kvs, q_pos, k_pos, place)


def natural_pieces(pieces, part, image_count):
    roles, seqs, tps = lax.axis_size("role"), lax.axis_size("seq"), lax.axis_size("tp")
    role, seq, tp = lax.axis_index("role"), lax.axis_index("seq"), lax.axis_index("tp")
    late, columns = pieces[0].shape
    by_source = jnp.stack(pieces)[jnp.arange(tps) ^ tp]
    text = jnp.transpose(by_source, (1, 0, 2))
    device = jnp.arange(roles * seqs)
    entry = ((device // seqs) ^ role) * seqs + ((device % seqs) ^ seq)
    image = by_source.reshape(tps, late, roles * seqs, part)[:, :, entry]
    image = jnp.transpose(image, (1, 2, 0, 3)).reshape(late, tps, columns)
    chosen = jnp.where(jnp.arange(late)[:, None, None] < image_count, image, text)
    return [jnp.take(chosen, tp ^ k, axis=1) for k in range(tps)]


def body(
    merger_hidden,
    merger_out,
    row_position,
    prompt_embeds,
    norm_gain,
    query_weight,
    key_weight,
    value_weight,
):
    roles, seqs, tps = lax.axis_size("role"), lax.axis_size("seq"), lax.axis_size("tp")
    role, seq, tp = lax.axis_index("role"), lax.axis_index("seq"), lax.axis_index("tp")
    groups = roles * seqs
    rank = role * seqs + seq
    row_count = merger_hidden.shape[0]
    tok_count, columns = prompt_embeds.shape
    strip = merger_out.shape[1]
    part = strip // tps
    late = groups * (2 * row_count // groups)
    early = tok_count - late

    def gather_rows(x):
        mine = jnp.concatenate(gather_xor(x, "seq"), axis=0)
        return jnp.concatenate(gather_xor(mine, "role"), axis=0)

    all_pos = gather_rows(row_position[:, None])[:, 0]
    valid = all_pos >= 0
    owner = jnp.where(valid, all_pos // tok_count, groups)
    lower = (owner[:, None] == owner[None, :]) & (all_pos[None, :] < all_pos[:, None])
    order = jnp.sum(lower.astype(jnp.int32), axis=1)
    device_of = [(role ^ r) * seqs + (seq ^ s) for r in range(roles) for s in range(seqs)]
    targets = jnp.stack(device_of)
    slot_order = jnp.arange(late, dtype=jnp.int32)
    route = (
        (owner[None, None, :] == targets[:, None, None])
        & (order[None, None, :] == slot_order[None, :, None])
    ).astype(BF16)

    tokens = rank * tok_count + jnp.arange(tok_count, dtype=jnp.int32)
    is_image = jnp.any(all_pos[None, :] == tokens[:, None], axis=1)
    earlier = jnp.arange(tok_count)[None, :] < jnp.arange(tok_count)[:, None]
    image_before = jnp.sum((earlier & is_image[None, :]).astype(jnp.int32), axis=1)
    text_before = jnp.arange(tok_count, dtype=jnp.int32) - image_before
    image_count = jnp.sum(is_image.astype(jnp.int32))
    slot = jnp.where(
        is_image,
        early + image_before,
        jnp.where(text_before < early, text_before, text_before + image_count),
    )
    placed = slot[None, :] == jnp.arange(tok_count, dtype=jnp.int32)[:, None]
    early_pick = placed[:early].astype(BF16)
    late_pick = (placed[early:] & ~is_image[None, :]).astype(BF16)
    slot_pos = jnp.sum(jnp.where(placed, tokens[None, :], 0), axis=1)

    early_own = dot(early_pick, prompt_embeds).astype(BF16)
    early_in = jnp.stack(gather_xor(early_own, "tp")[1:])
    gains = jnp.stack(gather_xor(norm_gain[None, :], "tp")).astype(F32)

    hidden = gather_rows(merger_hidden)
    partial_value = dot(hidden, merger_out)
    summed = lax.dynamic_slice_in_dim(partial_value, tp * part, part, axis=1)
    narrow = partial_value.astype(BF16)
    for k in range(1, tps):
        piece = lax.dynamic_slice_in_dim(narrow, (tp ^ k) * part, part, axis=1)
        summed = summed + swap(piece, "tp", k).astype(F32)
    embeds = summed.astype(BF16)

    routed = dot(route.reshape(groups * late, -1), embeds).astype(BF16)
    routed = routed.reshape(roles, seqs, late, part)
    by_role = [routed[0]] + [swap(routed[r], "role", r) for r in range(1, roles)]
    by_role = jnp.stack(by_role, axis=1)
    arrived = [by_role[0]] + [swap(by_role[s], "seq", s) for s in range(1, seqs)]
    image_rows = jnp.concatenate(
        [arrived[s][r] for r in range(roles) for s in range(seqs)], axis=1
    )
    late_own = image_rows + dot(late_pick, prompt_embeds).astype(BF16)
    late_pieces = gather_xor(late_own, "tp")
    if part % 128:
        late_pieces = natural_pieces(late_pieces, part, image_count)
    late_own, late_in = late_pieces[0], jnp.stack(late_pieces[1:])

    half = HEAD_DIM // 2
    frequency = 1000000.0 ** (-jnp.arange(half, dtype=F32) / half)
    angles = slot_pos.astype(F32)[:, None] * frequency[None, :]
    cosine = jnp.concatenate([jnp.cos(angles)] * 2, axis=1)
    sine = jnp.concatenate([-jnp.sin(angles), jnp.sin(angles)], axis=1)

    info = jnp.stack([tp, image_count] + device_of).astype(jnp.int32)
    queries, keys_values, late_rows = project(
        info, early_own, early_in, late_own, late_in, gains, cosine, sine,
        query_weight, key_weight, value_weight, groups,
    )

    local_kv = key_weight.shape[1] // HEAD_DIM
    place_image = (placed[early:] & is_image[None, :]).astype(BF16)
    stream = jnp.where(
        is_image[:, None],
        lax.dot_general(
            place_image, late_rows, (((0,), (0,)), ((), ())), preferred_element_type=F32
        ).astype(BF16),
        prompt_embeds,
    )

    heads_kv = keys_values.shape[1] // 2
    interleaved = jnp.concatenate(
        [
            keys_values[:, side * heads_kv + h * HEAD_DIM : side * heads_kv + (h + 1) * HEAD_DIM]
            for h in range(local_kv)
            for side in range(2)
        ],
        axis=1,
    )
    same_role = gather_xor(interleaved, "seq")
    kvs = list(same_role)
    stacked = jnp.stack(same_role)
    for r in range(1, roles):
        other = swap(stacked, "role", r, lambda a, b: a < b)
        kvs += [other[s] for s in range(seqs)]
    blocks = jnp.stack(device_of).astype(jnp.int32)
    context = attend(
        blocks, queries, kvs, slot_pos[:, None], slot_pos[None, :],
        placed.T.astype(BF16), local_kv,
    )
    return (stream, context)


def solution(mesh):
    in_specs = (
        P(("role", "seq"), "tp"),
        P("tp", ("role", "seq")),
        P(("role", "seq")),
        P(("role", "seq"), "tp"),
        P("tp"),
        P(None, "tp"),
        P(None, "tp"),
        P(None, "tp"),
    )
    out_specs = (P(("role", "seq"), "tp"), P(("role", "seq"), "tp"))
    return jax.shard_map(body, mesh=mesh, in_specs=in_specs, out_specs=out_specs, check_vma=False)
```

time: 305 us -> 161 us (0.53)
  blocking collectives: 114 us -> 0 us
  waiting for transfers between devices: 118 us -> 68 us
  starting transfers between devices: 7.98 us -> 41.1 us
  Pallas kernels: 0 us -> 26.8 us
  matrix products: 24.7 us -> 6.44 us
  between operations: 14 us -> 1.05 us
  local copies, waits for them, and re-layouts: 14.7 us -> 8.25 us
    all_gather x2 -> x0, waiting for transfers between devices: 75.7 us -> none  [the longest x1 49.5 us: body(): shard_piece = lax.all_gather(normed, 'tp', axis=1, tiled=True)]
    ppermute x0 -> x28, waiting for transfers between devices: none -> 68 us  [swap(): return lax.ppermute(x, axis, pairs)]
    all_gather x2 -> x0, blocking collectives: 53.1 us -> none  [the longest x1 26.6 us: body(): lax.all_gather(value_rows, ('role', 'seq'), axis=0, tiled=True)]
    all_to_all x1 -> x0, blocking collectives: 51.7 us -> none  [body(): lax.all_to_all(strips, ('role', 'seq'), split_axis=0, concat_axis=1, tile...]
    ppermute x0 -> x28, starting transfers between devices: none -> 41.1 us  [swap(): return lax.ppermute(x, axis, pairs)]
    reduce_scatter x1 -> x0, waiting for transfers between devices: 27.3 us -> none  [sum_hidden(): lax.psum_scatter(partial_value, 'tp', scatter_dimension=1, tiled=True)]
    pallas_call x0 -> x2, Pallas kernels: none -> 26.8 us  [the longest x1 15.6 us: project(): pl.pallas_call(functools.partial(qkv_kernel, tp, groups), grid_spec=pltpu...]
    dot_general x6 -> x5, matrix products: 24.7 us -> 6.44 us  [the longest x4 3.47 us: dot(): return jnp.dot(a, b, preferred_element_type=F32)]
  transfers between devices with their start and end apart: 5 -> 28, of which waited for: 4 -> 10; matrix products, arithmetic and copies ran while one was open for 2% -> 12% of each run, Pallas kernels for 0% -> 0%
where the time goes in v1:
time: 161 us; the launch traced here: 160 us
  waiting for transfers between devices  68 us (42%)
  starting transfers between devices  41.1 us (26%)
  Pallas kernels  26.8 us (17%)
  other arithmetic  8.77 us (5%)
  local copies, waits for them, and re-layouts  8.25 us (5%)
  matrix products  6.44 us (4%)
    ppermute x28, waiting for transfers between devices, swap(): return lax.ppermute(x, axis, pairs)  68 us
    ppermute x28, starting transfers between devices, swap(): return lax.ppermute(x, axis, pairs)  41.1 us
    pallas_call x1, Pallas kernels, project(): pl.pallas_call(functools.partial(qkv_kernel, tp, groups), grid_spec=pltpu...  15.6 us
    pallas_call x1, Pallas kernels, attend(): pl.pallas_call(functools.partial(attention_kernel, len(kvs), group_size),...  11.2 us
    dot_general x4, matrix products, dot(): return jnp.dot(a, b, preferred_element_type=F32)  3.47 us
  transfers between devices with their start and end apart: 28, of which 10 were waited for; matrix products, arithmetic and copies ran while one was open for 12% of the time, Pallas kernels for 0%

profile of v1, /device:TPU:0, one launch (start us, length us, event | category | flops | bytes accessed | tf_op | source)
XLA Modules:
  0.0 160.3 jit_solution(7439547022178130056)
XLA Ops:
  0.7 3.1 %collective-permute-start = (s32[64,1]{0,1:T(1,128)}, s32[64,1]{0,1:T(1,128)S(1)}, u32[]{:S(2)}, u32[]{:S(2)}) collective-permute-start(s32[64,1]{0,1:T(1,128)} %bitcast.100), channel_id=1, source_target_pairs={{0,4},{4,0},{8,12},{12,8},{1,5},{5,1},{9,13},{13,9},{2,6},{6,2},{1... | collective-permute-start | bytes 776 | tf_op jit(solution)/shard_map/ppermute | solution.py:19
  3.8 2.6 %collective-permute-start.1 = (s32[64,1]{0,1:T(1,128)}, s32[64,1]{0,1:T(1,128)S(1)}, u32[]{:S(2)}, u32[]{:S(2)}) collective-permute-start(s32[64,1]{0,1:T(1,128)} %bitcast.101), channel_id=1, source_target_pairs={{0,8},{4,12},{8,0},{12,4},{1,9},{5,13},{9,1},{13,5},{2,10},{6,14},... | collective-permute-start | bytes 776 | tf_op jit(solution)/shard_map/ppermute | solution.py:19
  6.4 0.9 collective-permute-start.7
  7.3 3.5 %collective-permute-start.8 = (bf16[64,1280]{1,0:T(8,128)(2,1)}, bf16[64,1280]{1,0:T(8,128)(2,1)S(1)}, u32[]{:S(2)}, u32[]{:S(2)}) collective-permute-start(bf16[64,1280]{1,0:T(8,128)(2,1)} %param.8), channel_id=1, source_target_pairs={{0,8},{4,12},{8,0},{12,4},{1,9},{5,13},{9,1},{13,5},{2,10},{6,14},... | collective-permute-start | bytes 491528 | tf_op jit(solution)/shard_map/ppermute | solution.py:19
  10.8 1.6 %constant_dynamic-update-slice_fusion.4 = bf16[512,1280]{1,0:T(8,128)(2,1)} fusion(bf16[64,1280]{1,0:T(8,128)(2,1)} %param.8), kind=kLoop, calls=%fused_computation.62 | loop fusion | bytes 327680
  12.4 0.7 broadcast_in_dim.27
  13.2 1.7 %collective-permute-start.21 = (bf16[1,2048]{1,0:T(2,128)(2,1)S(1)}, bf16[1,2048]{1,0:T(2,128)(2,1)S(1)}, u32[]{:S(2)}, u32[]{:S(2)}) collective-permute-start(bf16[1,2048]{1,0:T(2,128)(2,1)S(1)} %broadcast_in_dim.27), channel_id=1, source_target_pairs={{0,1},{1,0},{2,3},{3,2},{4,5},{5,4},{6,7},{7,6},{8,9},{9,8},{10,11... | collective-permute-start | bytes 12296 | tf_op jit(solution)/shard_map/ppermute | solution.py:19
  14.9 0.7 pad_add_fusion
  15.6 1.3 stack.134
  17.0 1.6 collective-permute-start.22
  18.6 0.7 concatenate.58
  19.3 0.2 compare_reduce_fusion
  19.5 0.7 convert_reduce_fusion.2
  20.2 0.1 convert_reduce_fusion.1
  20.3 0.7 concatenate.63
  21.1 0.3 convert_reduce_fusion
  21.5 0.2 broadcast_and_fusion
  21.8 0.6 fusion.26
  22.6 0.3 collective-permute-start.10
  23.0 1.8 %collective-permute-done.10 = bf16[256,1280]{1,0:T(8,128)(2,1)S(1)} collective-permute-done((bf16[256,1280]{1,0:T(8,128)(2,1)S(1)}, bf16[256,1280]{1,0:T(8,128)(2,1)S(1)}, u32[]{:S(2)}, u32[]{:S(2)}) %collective-permute-start.10) | collective-permute-done | bytes 655392 | tf_op jit(solution)/shard_map/ppermute | solution.py:19
  24.8 1.5 fusion.29
  26.4 0.1 constant_dynamic-slice_fusion.2
  26.5 1.2 collective-permute-start.11
  27.7 1.5 collective-permute-start.12
  29.2 0.9 collective-permute-start.13
  30.1 0.3 convolution_convert_fusion.2.early_own
  30.4 5.4 %collective-permute-done.11 = bf16[512,256]{1,0:T(8,128)(2,1)S(1)} collective-permute-done((bf16[512,256]{1,0:T(8,128)(2,1)S(1)}, bf16[512,256]{1,0:T(8,128)(2,1)S(1)}, u32[]{:S(2)}, u32[]{:S(2)}) %collective-permute-start.11) | collective-permute-done | bytes 262176 | tf_op jit(solution)/shard_map/ppermute | solution.py:19
  35.7 2.1 %collective-permute-start.23 = (bf16[1,2048]{1,0:T(2,128)(2,1)S(1)}, bf16[1,2048]{1,0:T(2,128)(2,1)S(1)}, u32[]{:S(2)}, u32[]{:S(2)}) collective-permute-start(bf16[1,2048]{1,0:T(2,128)(2,1)S(1)} %broadcast_in_dim.27), channel_id=1, source_target_pairs={{0,3},{1,2},{2,1},{3,0},{4,7},{5,6},{6,5},{7,4},{8,11},{9,10},{10,... | collective-permute-start | bytes 12296 | tf_op jit(solution)/shard_map/ppermute | solution.py:19
  37.8 3.7 %collective-permute-done.12 = bf16[512,256]{1,0:T(8,128)(2,1)S(1)} collective-permute-done((bf16[512,256]{1,0:T(8,128)(2,1)S(1)}, bf16[512,256]{1,0:T(8,128)(2,1)S(1)}, u32[]{:S(2)}, u32[]{:S(2)}) %collective-permute-start.12) | collective-permute-done | bytes 262176 | tf_op jit(solution)/shard_map/ppermute | solution.py:19
  41.5 0.5 convolution_convert_fusion.3
  42.2 0.1 select_reduce_fusion
  42.3 1.2 collective-permute-start.4
  43.5 0.5 fusion.19
  44.1 3.1 %collective-permute-start.15 = (bf16[2,128,256]{2,1,0:T(8,128)(2,1)S(1)}, bf16[2,128,256]{2,1,0:T(8,128)(2,1)S(1)}, u32[]{:S(2)}, u32[]{:S(2)}) collective-permute-start(bf16[2,128,256]{2,1,0:T(8,128)(2,1)S(1)} %get-tuple-element.17), channel_id=1, source_target_pairs={{0,4},{4,0},{8,12},{12,8},{1,5},{5,1},{9,13},{13,9},{2,6},{6,2},{1... | collective-permute-start | bytes 393224 | tf_op jit(solution)/shard_map/ppermute | solution.py:19
  47.2 3.9 %collective-permute-done.15 = bf16[2,128,256]{2,1,0:T(8,128)(2,1)S(1)} collective-permute-done((bf16[2,128,256]{2,1,0:T(8,128)(2,1)S(1)}, bf16[2,128,256]{2,1,0:T(8,128)(2,1)S(1)}, u32[]{:S(2)}, u32[]{:S(2)}) %collective-permute-start.15) | collective-permute-done | bytes 131104 | tf_op jit(solution)/shard_map/ppermute | solution.py:19
  51.1 2.6 %collective-permute-start.16 = (bf16[2,128,256]{2,1,0:T(8,128)(2,1)S(1)}, bf16[2,128,256]{2,1,0:T(8,128)(2,1)S(1)}, u32[]{:S(2)}, u32[]{:S(2)}) collective-permute-start(bf16[2,128,256]{2,1,0:T(8,128)(2,1)S(1)} %get-tuple-element.16), channel_id=1, source_target_pairs={{0,8},{4,12},{8,0},{12,4},{1,9},{5,13},{9,1},{13,5},{2,10},{6,14},... | collective-permute-start | bytes 393224 | tf_op jit(solution)/shard_map/ppermute | solution.py:19
  53.7 6.1 %collective-permute-done.16 = bf16[2,128,256]{2,1,0:T(8,128)(2,1)S(1)} collective-permute-done((bf16[2,128,256]{2,1,0:T(8,128)(2,1)S(1)}, bf16[2,128,256]{2,1,0:T(8,128)(2,1)S(1)}, u32[]{:S(2)}, u32[]{:S(2)}) %collective-permute-start.16) | collective-permute-done | bytes 131104 | tf_op jit(solution)/shard_map/ppermute | solution.py:19
  59.9 2.4 %collective-permute-start.17 = (bf16[2,128,256]{2,1,0:T(8,128)(2,1)S(1)}, bf16[2,128,256]{2,1,0:T(8,128)(2,1)S(1)}, u32[]{:S(2)}, u32[]{:S(2)}) collective-permute-start(bf16[2,128,256]{2,1,0:T(8,128)(2,1)S(1)} %get-tuple-element.15), channel_id=1, source_target_pairs={{0,12},{4,8},{8,4},{12,0},{1,13},{5,9},{9,5},{13,1},{2,14},{6,10},... | collective-permute-start | bytes 393224 | tf_op jit(solution)/shard_map/ppermute | solution.py:19
  62.3 4.4 %collective-permute-done.17 = bf16[2,128,256]{2,1,0:T(8,128)(2,1)S(1)} collective-permute-done((bf16[2,128,256]{2,1,0:T(8,128)(2,1)S(1)}, bf16[2,128,256]{2,1,0:T(8,128)(2,1)S(1)}, u32[]{:S(2)}, u32[]{:S(2)}) %collective-permute-start.17) | collective-permute-done | bytes 131104 | tf_op jit(solution)/shard_map/ppermute | solution.py:19
  66.6 1.0 collective-permute-start.5
  67.7 1.4 collective-permute-start.6
  69.1 1.1 fusion.1.late_own
  70.2 1.1 collective-permute-start.18
  71.4 1.0 collective-permute-start.19
  72.4 1.4 collective-permute-start.20
  73.7 0.1 pad_maximum_fusion.5
  73.9 0.7 stack.122.info
  74.6 0.8 maximum_convert_fusion.gain
  75.4 19.5 %collective-permute-done.5 = bf16[128,2048]{1,0:T(8,128)(2,1)} collective-permute-done((bf16[128,2048]{1,0:T(8,128)(2,1)S(1)}, bf16[128,2048]{1,0:T(8,128)(2,1)}, u32[]{:S(2)}, u32[]{:S(2)}) %collective-permute-start.5) | collective-permute-done | bytes 524320 | tf_op jit(solution)/shard_map/ppermute | solution.py:19
  94.9 1.5 pad_maximum_fusion.early_in
  96.4 15.9 %collective-permute-done.19 = bf16[128,2048]{1,0:T(8,128)(2,1)} collective-permute-done((bf16[128,2048]{1,0:T(8,128)(2,1)}, bf16[128,2048]{1,0:T(8,128)(2,1)}, u32[]{:S(2)}, u32[]{:S(2)}) %collective-permute-start.19) | collective-permute-done | bytes 524320 | tf_op jit(solution)/shard_map/ppermute | solution.py:19
  112.3 1.5 pad_maximum_fusion.1.late_in
  113.9 15.6 %shard_map.95 = (bf16[256,1024]{1,0:T(8,128)(2,1)S(1)}, bf16[256,256]{1,0:T(8,128)(2,1)S(1)}, bf16[128,2048]{1,0:T(8,128)(2,1)S(1)}) custom-call(s32[10]{0:T(128)S(1)} %stack.122.info, bf16[128,2048]{1,0:T(8,128)(2,1)S(1)} %convolution_convert_fusion.2.early_own, bf16[3,128,2048]{2,1,0:T(8,128)(2,1)S(1)} %pad_maximum_fusion.early_in, ...), custom_call_target="tpu_custom_call" | custom-call | tf_op jit(solution)/shard_map/pallas_call | solution.py:125
  129.4 0.8 copy-done.1
  130.2 2.5 %collective-permute-start.25 = (bf16[256,256]{1,0:T(8,128)(2,1)S(1)}, bf16[256,256]{1,0:T(8,128)(2,1)S(1)}, u32[]{:S(2)}, u32[]{:S(2)}) collective-permute-start(bf16[256,256]{1,0:T(8,128)(2,1)S(1)} %get-tuple-element.7.refs_0_), channel_id=1, source_target_pairs={{0,8},{4,12},{8,0},{12,4},{1,9},{5,13},{9,1},{13,5},{2,10},{6,14},... | collective-permute-start | bytes 393224 | tf_op jit(solution)/shard_map/ppermute | solution.py:19
  132.8 1.8 %collective-permute-start.26 = (bf16[256,256]{1,0:T(8,128)(2,1)S(1)}, bf16[256,256]{1,0:T(8,128)(2,1)S(1)}, u32[]{:S(2)}, u32[]{:S(2)}) collective-permute-start(bf16[256,256]{1,0:T(8,128)(2,1)S(1)} %get-tuple-element.7.refs_0_), channel_id=1, source_target_pairs={{0,12},{4,8},{8,4},{12,0},{1,13},{5,9},{9,5},{13,1},{2,14},{6,10},... | collective-permute-start | bytes 393224 | tf_op jit(solution)/shard_map/ppermute | solution.py:19
  134.6 1.3 collective-permute-done.24.refs_1_
  136.0 5.9 %collective-permute-done.25.refs_2_ = bf16[256,256]{1,0:T(8,128)(2,1)S(1)} collective-permute-done((bf16[256,256]{1,0:T(8,128)(2,1)S(1)}, bf16[256,256]{1,0:T(8,128)(2,1)S(1)}, u32[]{:S(2)}, u32[]{:S(2)}) %collective-permute-start.25) | collective-permute-done | bytes 131104 | tf_op jit(solution)/shard_map/ppermute | solution.py:19
  141.9 0.9 pad_maximum_fusion.3
  142.8 2.1 %collective-permute-start.27 = (bf16[4,256,256]{2,1,0:T(8,128)(2,1)}, bf16[4,256,256]{2,1,0:T(8,128)(2,1)}, u32[]{:S(2)}, u32[]{:S(2)}) collective-permute-start(bf16[4,256,256]{2,1,0:T(8,128)(2,1)} %pad_maximum_fusion.3), channel_id=1, source_target_pairs={{0,16},{1,17},{2,18},{3,19},{4,20},{5,21},{6,22},{7,23},{8,24},{9,... | collective-permute-start | bytes 1572872 | tf_op jit(solution)/shard_map/ppermute | solution.py:19
  144.8 0.1 copy.11.refs_8_
  145.0 3.0 %fusion = bf16[256,2048]{1,0:T(8,128)(2,1)} fusion(bf16[256,2048]{1,0:T(8,128)(2,1)} %param.11, bf16[128,2048]{1,0:T(8,128)(2,1)} %copy-done.3, pred[256]{0:T(512)(128)(4,1)S(1)} %compare_reduce_fusion, pred[256,256]{1,0:T(32,128)(4,1)} %copy-done.9), kind=kOutput, calls=%fused_computation.1 | convolution fusion | flops 135299072 | bytes 2655232 | tf_op jit(solution)/shard_map/dot_general | solution.py:327
  148.0 1.1 slice_bitcast_fusion
  149.1 11.2 %shard_map.96 = bf16[256,1024]{1,0:T(8,128)(2,1)} custom-call(s32[8]{0:T(128)S(1)} %stack.127.blocks, bf16[256,1024]{1,0:T(8,128)(2,1)S(1)} %copy-done.2, bf16[256,256]{1,0:T(8,128)(2,1)S(1)} %copy-done.5, bf16[256,256]{1,0:T(8,128)(2,1)S(1)} %collective-permute-done.24.refs_1_, bf16[256,256]{1,0:T(8,128)(2,1)S(1)} %collective-permute-done.25.refs_2_, ...), custom_call_target="tpu_custom_call" | custom-call | tf_op jit(solution)/shard_map/pallas_call | solution.py:200
  (74 shorter events, 0.8 us)
Async XLA Ops:
  0.6 24.2 %copy-start = (bf16[1280,1024]{1,0:T(8,128)(2,1)S(1)}, bf16[1280,1024]{1,0:T(8,128)(2,1)}, u32[]{:S(2)}) copy-start(bf16[1280,1024]{1,0:T(8,128)(2,1)} %param.9) | copy-start | bytes 7864324
  0.6 21.9 %copy-start.7 = (bf16[64,1280]{1,0:T(8,128)(2,1)S(1)}, bf16[64,1280]{1,0:T(8,128)(2,1)}, u32[]{:S(2)}) copy-start(bf16[64,1280]{1,0:T(8,128)(2,1)} %param.8) | copy-start | bytes 491524
  0.7 12.4 %collective-permute-start = (s32[64,1]{0,1:T(1,128)}, s32[64,1]{0,1:T(1,128)S(1)}, u32[]{:S(2)}, u32[]{:S(2)}) collective-permute-start(s32[64,1]{0,1:T(1,128)} %bitcast.100), channel_id=1, source_target_pairs={{0,4},{4,0},{8,12},{12,8},{1,5},{5,1},{9,13},{13,9},{2,6},{6,2},{1... | collective-permute-start | bytes 776 | tf_op jit(solution)/shard_map/ppermute | solution.py:19
  3.8 9.4 %collective-permute-start.1 = (s32[64,1]{0,1:T(1,128)}, s32[64,1]{0,1:T(1,128)S(1)}, u32[]{:S(2)}, u32[]{:S(2)}) collective-permute-start(s32[64,1]{0,1:T(1,128)} %bitcast.101), channel_id=1, source_target_pairs={{0,8},{4,12},{8,0},{12,4},{1,9},{5,13},{9,1},{13,5},{2,10},{6,14},... | collective-permute-start | bytes 776 | tf_op jit(solution)/shard_map/ppermute | solution.py:19
  6.4 8.5 %collective-permute-start.2 = (s32[64,1]{0,1:T(1,128)}, s32[64,1]{0,1:T(1,128)S(1)}, u32[]{:S(2)}, u32[]{:S(2)}) collective-permute-start(s32[64,1]{0,1:T(1,128)} %bitcast.102), channel_id=1, source_target_pairs={{0,12},{4,8},{8,4},{12,0},{1,13},{5,9},{9,5},{13,1},{2,14},{6,10},... | collective-permute-start | bytes 776 | tf_op jit(solution)/shard_map/ppermute | solution.py:19
  6.4 16.2 %collective-permute-start.7 = (bf16[64,1280]{1,0:T(8,128)(2,1)}, bf16[64,1280]{1,0:T(8,128)(2,1)S(1)}, u32[]{:S(2)}, u32[]{:S(2)}) collective-permute-start(bf16[64,1280]{1,0:T(8,128)(2,1)} %param.8), channel_id=1, source_target_pairs={{0,4},{4,0},{8,12},{12,8},{1,5},{5,1},{9,13},{13,9},{2,6},{6,2},{1... | collective-permute-start | bytes 491528 | tf_op jit(solution)/shard_map/ppermute | solution.py:19
  7.3 15.3 %collective-permute-start.8 = (bf16[64,1280]{1,0:T(8,128)(2,1)}, bf16[64,1280]{1,0:T(8,128)(2,1)S(1)}, u32[]{:S(2)}, u32[]{:S(2)}) collective-permute-start(bf16[64,1280]{1,0:T(8,128)(2,1)} %param.8), channel_id=1, source_target_pairs={{0,8},{4,12},{8,0},{12,4},{1,9},{5,13},{9,1},{13,5},{2,10},{6,14},... | collective-permute-start | bytes 491528 | tf_op jit(solution)/shard_map/ppermute | solution.py:19
  13.1 9.5 %collective-permute-start.9 = (bf16[64,1280]{1,0:T(8,128)(2,1)}, bf16[64,1280]{1,0:T(8,128)(2,1)S(1)}, u32[]{:S(2)}, u32[]{:S(2)}) collective-permute-start(bf16[64,1280]{1,0:T(8,128)(2,1)} %param.8), channel_id=1, source_target_pairs={{0,12},{4,8},{8,4},{12,0},{1,13},{5,9},{9,5},{13,1},{2,14},{6,10},... | collective-permute-start | bytes 491528 | tf_op jit(solution)/shard_map/ppermute | solution.py:19
  13.2 54.5 %collective-permute-start.21 = (bf16[1,2048]{1,0:T(2,128)(2,1)S(1)}, bf16[1,2048]{1,0:T(2,128)(2,1)S(1)}, u32[]{:S(2)}, u32[]{:S(2)}) collective-permute-start(bf16[1,2048]{1,0:T(2,128)(2,1)S(1)} %broadcast_in_dim.27), channel_id=1, source_target_pairs={{0,1},{1,0},{2,3},{3,2},{4,5},{5,4},{6,7},{7,6},{8,9},{9,8},{10,11... | collective-permute-start | bytes 12296 | tf_op jit(solution)/shard_map/ppermute | solution.py:19
  15.6 1.4 collective-permute-start.3
  17.0 53.2 %collective-permute-start.22 = (bf16[1,2048]{1,0:T(2,128)(2,1)S(1)}, bf16[1,2048]{1,0:T(2,128)(2,1)S(1)}, u32[]{:S(2)}, u32[]{:S(2)}) collective-permute-start(bf16[1,2048]{1,0:T(2,128)(2,1)S(1)} %broadcast_in_dim.27), channel_id=1, source_target_pairs={{0,2},{1,3},{2,0},{3,1},{4,6},{5,7},{6,4},{7,5},{8,10},{9,11},{10,... | collective-permute-start | bytes 12296 | tf_op jit(solution)/shard_map/ppermute | solution.py:19
  21.0 1.9 %copy-start.10 = (bf16[512,1280]{1,0:T(8,128)(2,1)S(1)}, bf16[512,1280]{1,0:T(8,128)(2,1)}, u32[]{:S(2)}) copy-start(bf16[512,1280]{1,0:T(8,128)(2,1)} %constant_dynamic-update-slice_fusion.4) | copy-start | bytes 3932164
  22.5 46.6 %copy-start.9 = (pred[256,256]{1,0:T(32,128)(4,1)}, pred[256,256]{1,0:T(32,128)(4,1)S(1)}, u32[]{:S(2)}) copy-start(pred[256,256]{1,0:T(32,128)(4,1)S(1)} %get-tuple-element.24) | copy-start | bytes 196612
  22.6 2.2 %collective-permute-start.10 = (bf16[256,1280]{1,0:T(8,128)(2,1)S(1)}, bf16[256,1280]{1,0:T(8,128)(2,1)S(1)}, u32[]{:S(2)}, u32[]{:S(2)}) collective-permute-start(bf16[256,1280]{1,0:T(8,128)(2,1)S(1)} %pad_maximum_fusion.2), channel_id=1, source_target_pairs={{0,16},{16,0},{1,17},{17,1},{2,18},{18,2},{3,19},{19,3},{4,20},{20... | collective-permute-start | bytes 1966088 | tf_op jit(solution)/shard_map/ppermute | solution.py:19
  26.4 3.7 %copy-start.6 = (bf16[256,2048]{1,0:T(8,128)(2,1)S(1)}, bf16[256,2048]{1,0:T(8,128)(2,1)}, u32[]{:S(2)}) copy-start(bf16[256,2048]{1,0:T(8,128)(2,1)} %param.11) | copy-start | bytes 3145732
  26.5 9.2 %collective-permute-start.11 = (bf16[512,256]{1,0:T(8,128)(2,1)S(1)}, bf16[512,256]{1,0:T(8,128)(2,1)S(1)}, u32[]{:S(2)}, u32[]{:S(2)}) collective-permute-start(bf16[512,256]{1,0:T(8,128)(2,1)S(1)} %get-tuple-element.8), channel_id=1, source_target_pairs={{0,1},{1,0},{2,3},{3,2},{4,5},{5,4},{6,7},{7,6},{8,9},{9,8},{10,11... | collective-permute-start | bytes 786440 | tf_op jit(solution)/shard_map/ppermute | solution.py:19
  27.7 13.9 %collective-permute-start.12 = (bf16[512,256]{1,0:T(8,128)(2,1)S(1)}, bf16[512,256]{1,0:T(8,128)(2,1)S(1)}, u32[]{:S(2)}, u32[]{:S(2)}) collective-permute-start(bf16[512,256]{1,0:T(8,128)(2,1)S(1)} %get-tuple-element.10), channel_id=1, source_target_pairs={{0,2},{1,3},{2,0},{3,1},{4,6},{5,7},{6,4},{7,5},{8,10},{9,11},{10,... | collective-permute-start | bytes 786440 | tf_op jit(solution)/shard_map/ppermute | solution.py:19
  29.2 12.3 %collective-permute-start.13 = (bf16[512,256]{1,0:T(8,128)(2,1)S(1)}, bf16[512,256]{1,0:T(8,128)(2,1)S(1)}, u32[]{:S(2)}, u32[]{:S(2)}) collective-permute-start(bf16[512,256]{1,0:T(8,128)(2,1)S(1)} %get-tuple-element.9), channel_id=1, source_target_pairs={{0,3},{1,2},{2,1},{3,0},{4,7},{5,6},{6,5},{7,4},{8,11},{9,10},{10,... | collective-permute-start | bytes 786440 | tf_op jit(solution)/shard_map/ppermute | solution.py:19
  35.7 35.6 %collective-permute-start.23 = (bf16[1,2048]{1,0:T(2,128)(2,1)S(1)}, bf16[1,2048]{1,0:T(2,128)(2,1)S(1)}, u32[]{:S(2)}, u32[]{:S(2)}) collective-permute-start(bf16[1,2048]{1,0:T(2,128)(2,1)S(1)} %broadcast_in_dim.27), channel_id=1, source_target_pairs={{0,3},{1,2},{2,1},{3,0},{4,7},{5,6},{6,5},{7,4},{8,11},{9,10},{10,... | collective-permute-start | bytes 12296 | tf_op jit(solution)/shard_map/ppermute | solution.py:19
  42.1 2.0 %collective-permute-start.14 = (bf16[4,128,256]{2,1,0:T(8,128)(2,1)S(1)}, bf16[4,128,256]{2,1,0:T(8,128)(2,1)S(1)}, u32[]{:S(2)}, u32[]{:S(2)}) collective-permute-start(bf16[4,128,256]{2,1,0:T(8,128)(2,1)S(1)} %bitcast.93), channel_id=1, source_target_pairs={{0,16},{16,0},{1,17},{17,1},{2,18},{18,2},{3,19},{19,3},{4,20},{20... | collective-permute-start | bytes 786440 | tf_op jit(solution)/shard_map/ppermute | solution.py:19
  42.3 30.1 %collective-permute-start.4 = (bf16[128,2048]{1,0:T(8,128)(2,1)S(1)}, bf16[128,2048]{1,0:T(8,128)(2,1)S(1)}, u32[]{:S(2)}, u32[]{:S(2)}) collective-permute-start(bf16[128,2048]{1,0:T(8,128)(2,1)S(1)} %convolution_convert_fusion.2.early_own), channel_id=1, source_target_pairs={{0,1},{1,0},{2,3},{3,2},{4,5},{5,4},{6,7},{7,6},{8,9},{9,8},{10,11... | collective-permute-start | bytes 1572872 | tf_op jit(solution)/shard_map/ppermute | solution.py:19
  44.1 7.0 %collective-permute-start.15 = (bf16[2,128,256]{2,1,0:T(8,128)(2,1)S(1)}, bf16[2,128,256]{2,1,0:T(8,128)(2,1)S(1)}, u32[]{:S(2)}, u32[]{:S(2)}) collective-permute-start(bf16[2,128,256]{2,1,0:T(8,128)(2,1)S(1)} %get-tuple-element.17), channel_id=1, source_target_pairs={{0,4},{4,0},{8,12},{12,8},{1,5},{5,1},{9,13},{13,9},{2,6},{6,2},{1... | collective-permute-start | bytes 393224 | tf_op jit(solution)/shard_map/ppermute | solution.py:19
  51.1 8.7 %collective-permute-start.16 = (bf16[2,128,256]{2,1,0:T(8,128)(2,1)S(1)}, bf16[2,128,256]{2,1,0:T(8,128)(2,1)S(1)}, u32[]{:S(2)}, u32[]{:S(2)}) collective-permute-start(bf16[2,128,256]{2,1,0:T(8,128)(2,1)S(1)} %get-tuple-element.16), channel_id=1, source_target_pairs={{0,8},{4,12},{8,0},{12,4},{1,9},{5,13},{9,1},{13,5},{2,10},{6,14},... | collective-permute-start | bytes 393224 | tf_op jit(solution)/shard_map/ppermute | solution.py:19
  59.9 6.8 %collective-permute-start.17 = (bf16[2,128,256]{2,1,0:T(8,128)(2,1)S(1)}, bf16[2,128,256]{2,1,0:T(8,128)(2,1)S(1)}, u32[]{:S(2)}, u32[]{:S(2)}) collective-permute-start(bf16[2,128,256]{2,1,0:T(8,128)(2,1)S(1)} %get-tuple-element.15), channel_id=1, source_target_pairs={{0,12},{4,8},{8,4},{12,0},{1,13},{5,9},{9,5},{13,1},{2,14},{6,10},... | collective-permute-start | bytes 393224 | tf_op jit(solution)/shard_map/ppermute | solution.py:19
  66.6 28.2 %collective-permute-start.5 = (bf16[128,2048]{1,0:T(8,128)(2,1)S(1)}, bf16[128,2048]{1,0:T(8,128)(2,1)}, u32[]{:S(2)}, u32[]{:S(2)}) collective-permute-start(bf16[128,2048]{1,0:T(8,128)(2,1)S(1)} %convolution_convert_fusion.2.early_own), channel_id=1, source_target_pairs={{0,2},{1,3},{2,0},{3,1},{4,6},{5,7},{6,4},{7,5},{8,10},{9,11},{10,... | collective-permute-start | bytes 1572872 | tf_op jit(solution)/shard_map/ppermute | solution.py:19
  67.7 6.0 %copy-start.11 = (bf16[1,2048]{1,0:T(2,128)(2,1)}, bf16[1,2048]{1,0:T(2,128)(2,1)S(1)}, u32[]{:S(2)}) copy-start(bf16[1,2048]{1,0:T(2,128)(2,1)S(1)} %collective-permute-done.21) | copy-start | bytes 12292
  67.7 27.2 %collective-permute-start.6 = (bf16[128,2048]{1,0:T(8,128)(2,1)S(1)}, bf16[128,2048]{1,0:T(8,128)(2,1)}, u32[]{:S(2)}, u32[]{:S(2)}) collective-permute-start(bf16[128,2048]{1,0:T(8,128)(2,1)S(1)} %convolution_convert_fusion.2.early_own), channel_id=1, source_target_pairs={{0,3},{1,2},{2,1},{3,0},{4,7},{5,6},{6,5},{7,4},{8,11},{9,10},{10,... | collective-permute-start | bytes 1572872 | tf_op jit(solution)/shard_map/ppermute | solution.py:19
  70.2 3.5 %copy-start.12 = (bf16[1,2048]{1,0:T(2,128)(2,1)}, bf16[1,2048]{1,0:T(2,128)(2,1)S(1)}, u32[]{:S(2)}) copy-start(bf16[1,2048]{1,0:T(2,128)(2,1)S(1)} %collective-permute-done.22) | copy-start | bytes 12292
  70.2 26.2 %collective-permute-start.18 = (bf16[128,2048]{1,0:T(8,128)(2,1)}, bf16[128,2048]{1,0:T(8,128)(2,1)}, u32[]{:S(2)}, u32[]{:S(2)}) collective-permute-start(bf16[128,2048]{1,0:T(8,128)(2,1)} %fusion.1.late_own), channel_id=1, source_target_pairs={{0,1},{1,0},{2,3},{3,2},{4,5},{5,4},{6,7},{7,6},{8,9},{9,8},{10,11... | collective-permute-start | bytes 1572872 | tf_op jit(solution)/shard_map/ppermute | solution.py:19
  71.4 2.4 %copy-start.13 = (bf16[1,2048]{1,0:T(2,128)(2,1)}, bf16[1,2048]{1,0:T(2,128)(2,1)S(1)}, u32[]{:S(2)}) copy-start(bf16[1,2048]{1,0:T(2,128)(2,1)S(1)} %collective-permute-done.23) | copy-start | bytes 12292
  71.4 41.0 %collective-permute-start.19 = (bf16[128,2048]{1,0:T(8,128)(2,1)}, bf16[128,2048]{1,0:T(8,128)(2,1)}, u32[]{:S(2)}, u32[]{:S(2)}) collective-permute-start(bf16[128,2048]{1,0:T(8,128)(2,1)} %fusion.1.late_own), channel_id=1, source_target_pairs={{0,2},{1,3},{2,0},{3,1},{4,6},{5,7},{6,4},{7,5},{8,10},{9,11},{10,... | collective-permute-start | bytes 1572872 | tf_op jit(solution)/shard_map/ppermute | solution.py:19
  72.4 1.5 copy-start.8
  72.4 40.0 %collective-permute-start.20 = (bf16[128,2048]{1,0:T(8,128)(2,1)}, bf16[128,2048]{1,0:T(8,128)(2,1)}, u32[]{:S(2)}, u32[]{:S(2)}) collective-permute-start(bf16[128,2048]{1,0:T(8,128)(2,1)} %fusion.1.late_own), channel_id=1, source_target_pairs={{0,3},{1,2},{2,1},{3,0},{4,7},{5,6},{6,5},{7,4},{8,11},{9,10},{10,... | collective-permute-start | bytes 1572872 | tf_op jit(solution)/shard_map/ppermute | solution.py:19
  129.4 0.8 copy-start.1
  130.2 14.6 %copy-start.3 = (bf16[128,2048]{1,0:T(8,128)(2,1)}, bf16[128,2048]{1,0:T(8,128)(2,1)S(1)}, u32[]{:S(2)}) copy-start(bf16[128,2048]{1,0:T(8,128)(2,1)S(1)} %get-tuple-element.5) | copy-start | bytes 1572868
  130.2 14.6 %copy-start.4 = (bf16[256,256]{1,0:T(8,128)(2,1)}, bf16[256,256]{1,0:T(8,128)(2,1)S(1)}, u32[]{:S(2)}) copy-start(bf16[256,256]{1,0:T(8,128)(2,1)S(1)} %get-tuple-element.7.refs_0_) | copy-start | bytes 393220
  130.2 5.7 %collective-permute-start.24 = (bf16[256,256]{1,0:T(8,128)(2,1)S(1)}, bf16[256,256]{1,0:T(8,128)(2,1)S(1)}, u32[]{:S(2)}, u32[]{:S(2)}) collective-permute-start(bf16[256,256]{1,0:T(8,128)(2,1)S(1)} %get-tuple-element.7.refs_0_), channel_id=1, source_target_pairs={{0,4},{4,0},{8,12},{12,8},{1,5},{5,1},{9,13},{13,9},{2,6},{6,2},{1... | collective-permute-start | bytes 393224 | tf_op jit(solution)/shard_map/ppermute | solution.py:19
  130.2 11.6 %collective-permute-start.25 = (bf16[256,256]{1,0:T(8,128)(2,1)S(1)}, bf16[256,256]{1,0:T(8,128)(2,1)S(1)}, u32[]{:S(2)}, u32[]{:S(2)}) collective-permute-start(bf16[256,256]{1,0:T(8,128)(2,1)S(1)} %get-tuple-element.7.refs_0_), channel_id=1, source_target_pairs={{0,8},{4,12},{8,0},{12,4},{1,9},{5,13},{9,1},{13,5},{2,10},{6,14},... | collective-permute-start | bytes 393224 | tf_op jit(solution)/shard_map/ppermute | solution.py:19
  132.8 9.1 %collective-permute-start.26 = (bf16[256,256]{1,0:T(8,128)(2,1)S(1)}, bf16[256,256]{1,0:T(8,128)(2,1)S(1)}, u32[]{:S(2)}, u32[]{:S(2)}) collective-permute-start(bf16[256,256]{1,0:T(8,128)(2,1)S(1)} %get-tuple-element.7.refs_0_), channel_id=1, source_target_pairs={{0,12},{4,8},{8,4},{12,0},{1,13},{5,9},{9,5},{13,1},{2,14},{6,10},... | collective-permute-start | bytes 393224 | tf_op jit(solution)/shard_map/ppermute | solution.py:19
  142.8 5.2 %collective-permute-start.27 = (bf16[4,256,256]{2,1,0:T(8,128)(2,1)}, bf16[4,256,256]{2,1,0:T(8,128)(2,1)}, u32[]{:S(2)}, u32[]{:S(2)}) collective-permute-start(bf16[4,256,256]{2,1,0:T(8,128)(2,1)} %pad_maximum_fusion.3), channel_id=1, source_target_pairs={{0,16},{1,17},{2,18},{3,19},{4,20},{5,21},{6,22},{7,23},{8,24},{9,... | collective-permute-start | bytes 1572872 | tf_op jit(solution)/shard_map/ppermute | solution.py:19
  145.0 4.1 %copy-start.2 = (bf16[256,1024]{1,0:T(8,128)(2,1)S(1)}, bf16[256,1024]{1,0:T(8,128)(2,1)}, u32[]{:S(2)}) copy-start(bf16[256,1024]{1,0:T(8,128)(2,1)} %copy-done.1) | copy-start | bytes 1572868
  145.0 4.1 %copy-start.5 = (bf16[256,256]{1,0:T(8,128)(2,1)S(1)}, bf16[256,256]{1,0:T(8,128)(2,1)}, u32[]{:S(2)}) copy-start(bf16[256,256]{1,0:T(8,128)(2,1)} %copy-done.4) | copy-start | bytes 393220
